TPU v7x, 32 devices: a whole 2x2x4 slice. The times are simulated.
32 devices in a mesh: pb: 8 (over y, x, core), wa: 4 (over z).
Axes of the slice: x: 2, y: 2, z: 4, core: 2. Of those that a mesh axis runs over, the one named last changes fastest.
Arguments:
- acts: bfloat16 [2048, 28672], P('pb', 'wa'), may hold values from -6 to 6
- grads: bfloat16 [2048, 8192], P('pb', 'wa'), may hold values from -6 to 6
- query_in: bfloat16 [28672, 4096], P('wa', 'pb'), may hold values from -0.03125 to 0.03125
- query_out: bfloat16 [8192, 4096], P('wa', 'pb'), may hold values from -0.01171875 to 0.01171875
- lengths: int32 [128], replicated, may hold values from 1 to 128, 2048 in all
Outputs:
- seq_scores: float32 [128, 128], P('pb', 'wa')
Inputs may be any that keep to these rules, and one draw needn't show every extreme that they name: The lengths sum to 2048 and the longest is exactly 128.
All inputs are finite; a program needn't handle non-finite values.
Results may differ from a plain program's by a relative error of at most 0.0003.
Values may be sent and summed in bfloat16 or wider, within the bound.
A program may use at most 64 MiB of HBM per device.

v0:
```python
import jax
import jax.numpy as jnp
from jax import lax
from jax.sharding import PartitionSpec as P

RANK = 32


def shifted(value, axis, steps):
    count = lax.axis_size(axis)
    pairs = [(source, (source + steps) % count) for source in range(count)]
    return lax.ppermute(value, axis, pairs)


def member_table(lengths, first, count):
    ends = jnp.cumsum(lengths)
    starts = ends - lengths
    spots = first + lax.iota(jnp.int32, count)
    inside = (spots[:, None] >= starts[None, :]) & (spots[:, None] < ends[None, :])
    return inside.astype(jnp.float32)


def query_scores(proj_in, proj_out):
    count = proj_in.shape[0]
    return jnp.sum((proj_in * proj_out).reshape(count, -1, RANK), axis=2)


def project(held):
    return (
        jnp.dot(held[0], held[2], preferred_element_type=jnp.float32),
        jnp.dot(held[1], held[3], preferred_element_type=jnp.float32),
    )


def advance(held):
    moved = shifted((held[0], held[1]), "pb", 1)
    return (moved[0], moved[1], held[2], held[3])


def shards(acts, grads, query_in, query_out, lengths):
    groups = lax.axis_size("pb")
    widths = lax.axis_size("wa")
    window = groups // 2
    group = lax.axis_index("pb")
    width_slot = lax.axis_index("wa")
    tok = acts.shape[0]
    share_rows = tok // widths
    local_q = query_in.shape[1] // RANK
    nseq = lengths.shape[0]
    totals = jnp.zeros((local_q, nseq), jnp.float32)

    def places(step):
        anchor = (group - step + groups) % groups
        return (anchor * tok + width_slot * share_rows, jnp.int32(0))

    def settle(totals, proj_in, proj_out, step):
        first, row = places(step)
        scores = query_scores(proj_in, proj_out)
        table = member_table(lengths, first, share_rows)
        contrib = jnp.dot(scores.T, table, precision=lax.Precision.HIGHEST)
        return totals + contrib

    held = (acts, grads, query_in, query_out)

    def settle_step(totals, held, step):
        proj_in, proj_out = project(held)
        summed = (
            lax.psum_scatter(proj_in, "wa", scatter_dimension=0, tiled=True),
            lax.psum_scatter(proj_out, "wa", scatter_dimension=0, tiled=True),
        )
        return settle(totals, summed[0], summed[1], step)

    def loop_body(step, carry):
        totals, held = carry
        totals = settle_step(totals, held, step)
        return (totals, advance(held))

    totals, held = lax.fori_loop(0, window - 1, loop_body, (totals, held))
    totals = settle_step(totals, held, jnp.int32(window - 1))
    share_seq = nseq // widths
    lengths_float = lengths.astype(jnp.float32)
    my_lengths = lax.dynamic_slice_in_dim(lengths_float, width_slot * share_seq, share_seq, 0)
    mine = lax.psum_scatter(totals, "wa", scatter_dimension=1, tiled=True)
    return mine / my_lengths[None, :]


def solution(mesh):
    return jax.shard_map(
        shards,
        mesh=mesh,
        in_specs=(P("pb", "wa"), P("pb", "wa"), P("wa", "pb"), P("wa", "pb"), P()),
        out_specs=P("pb", "wa"),
        check_vma=False,
    )
```

profile of v0, /device:TPU:0, one launch (start us, length us, event | category | flops | bytes accessed | tf_op | source)
XLA Modules:
  0.0 266.6 jit_solution(17890395542573217179)
XLA Ops:
  7.4 4.2 %copy.34 = bf16[256,7168]{1,0:T(8,128)(2,1)} copy(bf16[256,7168]{1,0:T(8,128)(2,1)} %param.7) | data formatting | bytes 7340032
  12.0 177.5 %while.20 = (s32[]{:T(128)}, f32[16,128]{1,0:T(8,128)S(1)}, bf16[256,7168]{1,0:T(8,128)(2,1)}, bf16[256,2048]{1,0:T(8,128)(2,1)S(1)}, bf16[7168,512]{1,0:T(8,128...) while((s32[]{:T(128)}, f32[16,128]{1,0:T(8,128)S(1)}, ...), condition=%wide.region_5.6_spmd.clone, body=%wide.region_1.5_spmd.clone.sunk | while | flops 2417585152 | bytes 56649708 | solution.py:78
  12.1 4.2 %copy.26 = bf16[256,7168]{1,0:T(8,128)(2,1)} copy(bf16[256,7168]{1,0:T(8,128)(2,1)} %get-tuple-element.403) | data formatting | bytes 7340032 | tf_op jit(solution)/shard_map/while
  17.0 1.5 fusion.42
  18.6 7.1 %fusion.41 = f32[256,512]{1,0:T(8,128)} fusion(bf16[256,7168]{1,0:T(8,128)(2,1)} %copy.26, bf16[7168,512]{1,0:T(8,128)(2,1)} %get-tuple-element.420), kind=kOutput, calls=%fused_computation.20.clone.1 | convolution fusion | flops 1879048192 | bytes 11534336 | tf_op jit(solution)/shard_map/while/body/eval_jaxpr/dot_general | solution.py:30
  25.7 2.6 collective-permute-start.1
  28.3 14.8 %reduce-scatter.16.cloned.1.call-done = f32[64,512]{1,0:T(8,128)} async-done(((f32[256,512]{1,0:T(8,128)}), f32[64,512]{1,0:T(8,128)}) %reduce-scatter.16.cloned.1.call-update) | async-done | bytes 131088 | tf_op jit(solution)/shard_map/while/body/eval_jaxpr/reduce_scatter | solution.py:69
  43.1 22.4 %reduce-scatter.14.cloned.1.call-done = f32[64,512]{1,0:T(8,128)} async-done(((f32[256,512]{1,0:T(8,128)}), f32[64,512]{1,0:T(8,128)}) %reduce-scatter.14.cloned.1.call-update) | async-done | bytes 131088 | tf_op jit(solution)/shard_map/while/body/eval_jaxpr/reduce_scatter | solution.py:68
  65.5 1.0 mul.47
  66.9 4.9 %collective-permute-done.1 = bf16[256,2048]{1,0:T(8,128)(2,1)S(1)} collective-permute-done((bf16[256,2048]{1,0:T(8,128)(2,1)S(1)}, bf16[256,2048]{1,0:T(8,128)(2,1)S(1)}, u32[]{:S(2)}, u32[]{:S(2)}) %collective-permute-start.1) | collective-permute-done | bytes 1048608 | tf_op jit(solution)/shard_map/while/body/eval_jaxpr/ppermute | solution.py:12
  71.7 4.2 %copy.26 = bf16[256,7168]{1,0:T(8,128)(2,1)} copy(bf16[256,7168]{1,0:T(8,128)(2,1)} %get-tuple-element.403) | data formatting | bytes 7340032 | tf_op jit(solution)/shard_map/while
  76.1 1.5 fusion.42
  77.7 7.1 %fusion.41 = f32[256,512]{1,0:T(8,128)} fusion(bf16[256,7168]{1,0:T(8,128)(2,1)} %copy.26, bf16[7168,512]{1,0:T(8,128)(2,1)} %get-tuple-element.420), kind=kOutput, calls=%fused_computation.20.clone.1 | convolution fusion | flops 1879048192 | bytes 11534336 | tf_op jit(solution)/shard_map/while/body/eval_jaxpr/dot_general | solution.py:30
  84.8 1.5 collective-permute-start.1
  86.3 15.6 %reduce-scatter.16.cloned.1.call-done = f32[64,512]{1,0:T(8,128)} async-done(((f32[256,512]{1,0:T(8,128)}), f32[64,512]{1,0:T(8,128)}) %reduce-scatter.16.cloned.1.call-update) | async-done | bytes 131088 | tf_op jit(solution)/shard_map/while/body/eval_jaxpr/reduce_scatter | solution.py:69
  101.9 22.3 %reduce-scatter.14.cloned.1.call-done = f32[64,512]{1,0:T(8,128)} async-done(((f32[256,512]{1,0:T(8,128)}), f32[64,512]{1,0:T(8,128)}) %reduce-scatter.14.cloned.1.call-update) | async-done | bytes 131088 | tf_op jit(solution)/shard_map/while/body/eval_jaxpr/reduce_scatter | solution.py:68
  124.2 1.0 mul.47
  125.6 5.0 %collective-permute-done.1 = bf16[256,2048]{1,0:T(8,128)(2,1)S(1)} collective-permute-done((bf16[256,2048]{1,0:T(8,128)(2,1)S(1)}, bf16[256,2048]{1,0:T(8,128)(2,1)S(1)}, u32[]{:S(2)}, u32[]{:S(2)}) %collective-permute-start.1) | collective-permute-done | bytes 1048608 | tf_op jit(solution)/shard_map/while/body/eval_jaxpr/ppermute | solution.py:12
  130.6 4.2 %copy.26 = bf16[256,7168]{1,0:T(8,128)(2,1)} copy(bf16[256,7168]{1,0:T(8,128)(2,1)} %get-tuple-element.403) | data formatting | bytes 7340032 | tf_op jit(solution)/shard_map/while
  135.0 1.5 fusion.42
  136.6 7.1 %fusion.41 = f32[256,512]{1,0:T(8,128)} fusion(bf16[256,7168]{1,0:T(8,128)(2,1)} %copy.26, bf16[7168,512]{1,0:T(8,128)(2,1)} %get-tuple-element.420), kind=kOutput, calls=%fused_computation.20.clone.1 | convolution fusion | flops 1879048192 | bytes 11534336 | tf_op jit(solution)/shard_map/while/body/eval_jaxpr/dot_general | solution.py:30
  144.3 16.6 %reduce-scatter.16.cloned.1.call-done = f32[64,512]{1,0:T(8,128)} async-done(((f32[256,512]{1,0:T(8,128)}), f32[64,512]{1,0:T(8,128)}) %reduce-scatter.16.cloned.1.call-update) | async-done | bytes 131088 | tf_op jit(solution)/shard_map/while/body/eval_jaxpr/reduce_scatter | solution.py:69
  160.8 22.3 %reduce-scatter.14.cloned.1.call-done = f32[64,512]{1,0:T(8,128)} async-done(((f32[256,512]{1,0:T(8,128)}), f32[64,512]{1,0:T(8,128)}) %reduce-scatter.14.cloned.1.call-update) | async-done | bytes 131088 | tf_op jit(solution)/shard_map/while/body/eval_jaxpr/reduce_scatter | solution.py:68
  183.1 1.0 mul.47
  184.5 5.0 %collective-permute-done.1 = bf16[256,2048]{1,0:T(8,128)(2,1)S(1)} collective-permute-done((bf16[256,2048]{1,0:T(8,128)(2,1)S(1)}, bf16[256,2048]{1,0:T(8,128)(2,1)S(1)}, u32[]{:S(2)}, u32[]{:S(2)}) %collective-permute-start.1) | collective-permute-done | bytes 1048608 | tf_op jit(solution)/shard_map/while/body/eval_jaxpr/ppermute | solution.py:12
  189.5 3.1 %fusion.16 = f32[256,512]{1,0:T(8,128)} fusion(bf16[256,2048]{1,0:T(8,128)(2,1)S(1)} %get-tuple-element.239, bf16[2048,512]{1,0:T(8,128)(2,1)} %get-tuple-element.455), kind=kOutput, calls=%fused_computation.23 | convolution fusion | flops 536870912 | bytes 3670016 | tf_op jit(solution)/shard_map/dot_general | solution.py:31
  192.7 7.1 %fusion.15 = f32[256,512]{1,0:T(8,128)} fusion(bf16[256,7168]{1,0:T(8,128)(2,1)} %get-tuple-element.238, bf16[7168,512]{1,0:T(8,128)(2,1)} %get-tuple-element.454), kind=kOutput, calls=%fused_computation.22 | convolution fusion | flops 1879048192 | bytes 11534336 | tf_op jit(solution)/shard_map/dot_general | solution.py:30
  199.8 15.7 %reduce-scatter.10.cloned.1.call-done = f32[64,512]{1,0:T(8,128)} async-done(((f32[256,512]{1,0:T(8,128)}), f32[64,512]{1,0:T(8,128)}) %reduce-scatter.10.cloned.1.call-update) | async-done | bytes 131088 | tf_op jit(solution)/shard_map/reduce_scatter | solution.py:69
  215.6 22.4 %reduce-scatter.8.cloned.1.call-done = f32[64,512]{1,0:T(8,128)} async-done(((f32[256,512]{1,0:T(8,128)}), f32[64,512]{1,0:T(8,128)}) %reduce-scatter.8.cloned.1.call-update) | async-done | bytes 131088 | tf_op jit(solution)/shard_map/reduce_scatter | solution.py:68
  237.9 1.0 mul.40
  240.1 17.5 %reduce-scatter.12.cloned.1.call-done = f32[32,16]{1,0:T(8,128)} async-done(((f32[128,16]{1,0:T(8,128)}), f32[32,16]{1,0:T(8,128)}) %reduce-scatter.12.cloned.1.call-update) | async-done | bytes 2064
  257.7 0.8 copy.17
  (63 shorter events, 5.2 us)
Async XLA Ops:
  7.4 4.2 %copy-start.1 = (s32[128]{0:T(128)S(1)}, s32[128]{0:T(128)}, u32[]{:S(2)}) copy-start(s32[128]{0:T(128)} %param.11) | copy-start | bytes 1540
  7.4 4.7 %copy-start = (bf16[256,2048]{1,0:T(8,128)(2,1)S(1)}, bf16[256,2048]{1,0:T(8,128)(2,1)}, u32[]{:S(2)}) copy-start(bf16[256,2048]{1,0:T(8,128)(2,1)} %param.8) | copy-start | bytes 3145732
  12.1 31.0 %reduce-scatter.16.cloned.1.call-start = ((), (), s32[]{:S(2)}) async-start(), calls=%async_computation.9 | async-start | bytes 655360 | tf_op jit(solution)/shard_map/while/body/eval_jaxpr/reduce_scatter | solution.py:69
  12.1 4.8 %copy-start.2 = (bf16[2048,512]{1,0:T(8,128)(2,1)S(1)}, bf16[2048,512]{1,0:T(8,128)(2,1)}, u32[]{:S(2)}) copy-start(bf16[2048,512]{1,0:T(8,128)(2,1)} %get-tuple-element.421) | copy-start | bytes 6291460 | tf_op jit(solution)/shard_map/while
  16.3 55.4 %collective-permute-start = (bf16[256,7168]{1,0:T(8,128)(2,1)}, bf16[256,7168]{1,0:T(8,128)(2,1)}, u32[]{:S(2)}, u32[]{:S(2)}) collective-permute-start(bf16[256,7168]{1,0:T(8,128)(2,1)} %copy.26), channel_id=1, source_target_pairs={{0,4},{4,8},{8,12},{12,16},{16,20},{20,24},{24,28},{28,0},{1,5},{5... | collective-permute-start | bytes 11010056 | tf_op jit(solution)/shard_map/while/body/eval_jaxpr/ppermute | solution.py:12
  18.5 47.0 %reduce-scatter.14.cloned.1.call-start = ((), (), s32[]{:S(2)}) async-start(), calls=%async_computation.8 | async-start | bytes 655360 | tf_op jit(solution)/shard_map/while/body/eval_jaxpr/reduce_scatter | solution.py:68
  25.7 46.1 %collective-permute-start.1 = (bf16[256,2048]{1,0:T(8,128)(2,1)S(1)}, bf16[256,2048]{1,0:T(8,128)(2,1)S(1)}, u32[]{:S(2)}, u32[]{:S(2)}) collective-permute-start(bf16[256,2048]{1,0:T(8,128)(2,1)S(1)} %copy.27), channel_id=1, source_target_pairs={{0,4},{4,8},{8,12},{12,16},{16,20},{20,24},{24,28},{28,0},{1,5},{5... | collective-permute-start | bytes 3145736 | tf_op jit(solution)/shard_map/while/body/eval_jaxpr/ppermute | solution.py:12
  71.7 30.2 %reduce-scatter.16.cloned.1.call-start = ((), (), s32[]{:S(2)}) async-start(), calls=%async_computation.9 | async-start | bytes 655360 | tf_op jit(solution)/shard_map/while/body/eval_jaxpr/reduce_scatter | solution.py:69
  71.7 4.3 %copy-start.2 = (bf16[2048,512]{1,0:T(8,128)(2,1)S(1)}, bf16[2048,512]{1,0:T(8,128)(2,1)}, u32[]{:S(2)}) copy-start(bf16[2048,512]{1,0:T(8,128)(2,1)} %get-tuple-element.421) | copy-start | bytes 6291460 | tf_op jit(solution)/shard_map/while
  76.0 54.7 %collective-permute-start = (bf16[256,7168]{1,0:T(8,128)(2,1)}, bf16[256,7168]{1,0:T(8,128)(2,1)}, u32[]{:S(2)}, u32[]{:S(2)}) collective-permute-start(bf16[256,7168]{1,0:T(8,128)(2,1)} %copy.26), channel_id=1, source_target_pairs={{0,4},{4,8},{8,12},{12,16},{16,20},{20,24},{24,28},{28,0},{1,5},{5... | collective-permute-start | bytes 11010056 | tf_op jit(solution)/shard_map/while/body/eval_jaxpr/ppermute | solution.py:12
  77.6 46.6 %reduce-scatter.14.cloned.1.call-start = ((), (), s32[]{:S(2)}) async-start(), calls=%async_computation.8 | async-start | bytes 655360 | tf_op jit(solution)/shard_map/while/body/eval_jaxpr/reduce_scatter | solution.py:68
  84.8 45.8 %collective-permute-start.1 = (bf16[256,2048]{1,0:T(8,128)(2,1)S(1)}, bf16[256,2048]{1,0:T(8,128)(2,1)S(1)}, u32[]{:S(2)}, u32[]{:S(2)}) collective-permute-start(bf16[256,2048]{1,0:T(8,128)(2,1)S(1)} %copy.27), channel_id=1, source_target_pairs={{0,4},{4,8},{8,12},{12,16},{16,20},{20,24},{24,28},{28,0},{1,5},{5... | collective-permute-start | bytes 3145736 | tf_op jit(solution)/shard_map/while/body/eval_jaxpr/ppermute | solution.py:12
  130.6 30.2 %reduce-scatter.16.cloned.1.call-start = ((), (), s32[]{:S(2)}) async-start(), calls=%async_computation.9 | async-start | bytes 655360 | tf_op jit(solution)/shard_map/while/body/eval_jaxpr/reduce_scatter | solution.py:69
  130.6 4.3 %copy-start.2 = (bf16[2048,512]{1,0:T(8,128)(2,1)S(1)}, bf16[2048,512]{1,0:T(8,128)(2,1)}, u32[]{:S(2)}) copy-start(bf16[2048,512]{1,0:T(8,128)(2,1)} %get-tuple-element.421) | copy-start | bytes 6291460 | tf_op jit(solution)/shard_map/while
  134.8 54.7 %collective-permute-start = (bf16[256,7168]{1,0:T(8,128)(2,1)}, bf16[256,7168]{1,0:T(8,128)(2,1)}, u32[]{:S(2)}, u32[]{:S(2)}) collective-permute-start(bf16[256,7168]{1,0:T(8,128)(2,1)} %copy.26), channel_id=1, source_target_pairs={{0,4},{4,8},{8,12},{12,16},{16,20},{20,24},{24,28},{28,0},{1,5},{5... | collective-permute-start | bytes 11010056 | tf_op jit(solution)/shard_map/while/body/eval_jaxpr/ppermute | solution.py:12
  136.5 46.6 %reduce-scatter.14.cloned.1.call-start = ((), (), s32[]{:S(2)}) async-start(), calls=%async_computation.8 | async-start | bytes 655360 | tf_op jit(solution)/shard_map/while/body/eval_jaxpr/reduce_scatter | solution.py:68
  143.7 45.8 %collective-permute-start.1 = (bf16[256,2048]{1,0:T(8,128)(2,1)S(1)}, bf16[256,2048]{1,0:T(8,128)(2,1)S(1)}, u32[]{:S(2)}, u32[]{:S(2)}) collective-permute-start(bf16[256,2048]{1,0:T(8,128)(2,1)S(1)} %copy.27), channel_id=1, source_target_pairs={{0,4},{4,8},{8,12},{12,16},{16,20},{20,24},{24,28},{28,0},{1,5},{5... | collective-permute-start | bytes 3145736 | tf_op jit(solution)/shard_map/while/body/eval_jaxpr/ppermute | solution.py:12
  189.5 26.1 %reduce-scatter.10.cloned.1.call-start = ((), (), s32[]{:S(2)}) async-start(), calls=%async_computation.6 | async-start | bytes 655360 | tf_op jit(solution)/shard_map/reduce_scatter | solution.py:69
  192.6 45.3 %reduce-scatter.8.cloned.1.call-start = ((), (), s32[]{:S(2)}) async-start(), calls=%async_computation.5 | async-start | bytes 655360 | tf_op jit(solution)/shard_map/reduce_scatter | solution.py:68
  199.8 57.9 %reduce-scatter.12.cloned.1.call-start = ((), (), s32[]{:S(2)}) async-start(), calls=%async_computation.7 | async-start | bytes 81920
Sparse Core Ops, SparseCore 0:
  18.6 24.3 reduce-scatter.15
  45.3 20.1 reduce-scatter.13
  77.7 24.1 reduce-scatter.15
  104.0 20.1 reduce-scatter.13
  136.6 24.1 reduce-scatter.15
  163.0 20.1 reduce-scatter.13
Sparse Core Ops, SparseCore 1:
  192.7 22.8 reduce-scatter.9
  217.7 20.2 reduce-scatter.7
  240.1 17.5 reduce-scatter.11
where the time goes:
time: 267 us
  waiting for transfers between devices  185 us (69%)
  matrix products  36.7 us (14%)
  local copies, waits for them, and re-layouts  19.4 us (7%)
  between operations  15.1 us (6%)
  starting transfers between devices  5.54 us (2%)
  other arithmetic  4.99 us (2%)
    reduce_scatter x4, waiting for transfers between devices, settle_step(): lax.psum_scatter(proj_in, 'wa', scatter_dimension=0, tiled=True)  89.4 us
    reduce_scatter x4, waiting for transfers between devices, settle_step(): lax.psum_scatter(proj_out, 'wa', scatter_dimension=0, tiled=True)  62.7 us
    dot_general x4, matrix products, project(): jnp.dot(held[0], held[2], preferred_element_type=jnp.float32)  28.3 us
    unnamed x4, waiting for transfers between devices  17.6 us
    ppermute x6, waiting for transfers between devices, shifted(): return lax.ppermute(value, axis, pairs)  14.9 us
    while x12, local copies, waits for them, and re-layouts  13 us
    dot_general x4, matrix products, project(): jnp.dot(held[1], held[3], preferred_element_type=jnp.float32)  7.67 us
    unnamed x8, local copies, waits for them, and re-layouts  5.79 us
  transfers between devices with their start and end apart: 15, of which 12 were waited for; matrix products, arithmetic and copies ran while one was open for 14% of the time, Pallas kernels for 0%

commit v1 on v0

v1 whole, which is shorter than its diff:
```python
import functools

import jax
import jax.numpy as jnp
from jax import lax
from jax.experimental import pallas as pl
from jax.experimental.pallas import tpu as pltpu
from jax.sharding import PartitionSpec as P

RANK = 32
MESH = pl.DeviceIdType.MESH
HIGHEST = lax.Precision.HIGHEST


def kernel(
    groups, widths, chunks,
    acts_ref, grads_ref, qin_ref, qout_ref, lengths_ref,
    out_ref,
    own_in, own_out, fac_in, fac_out, tok_in, tok_out,
    part, got, prods, table, tot, tot_got,
    load_sem, own_send, fwd_send, relay_send, tok_recv,
    part_send, part_recv, tot_send, tot_recv,
):
    window = groups // 2
    chips = groups // 2
    half = window // 2
    tok = acts_ref.shape[0]
    rows = tok // chunks
    share = rows // widths
    cols = qin_ref.shape[1]
    nseq = lengths_ref.shape[1]
    slots = window - 1

    g = lax.axis_index("pb")
    w = lax.axis_index("wa")
    core = lax.rem(g, 2)
    chip = g // 2
    even_core = core == 0
    odd_chip = lax.rem(chip, 2) == 1

    def device(chip_at, core_at):
        return lax.rem(chip_at + chips, chips) * 2 + core_at

    partner = chip * 2 + 1 - core

    loads = [
        pltpu.make_async_copy(acts_ref, own_in, load_sem.at[0]),
        pltpu.make_async_copy(qin_ref, fac_in, load_sem.at[1]),
        pltpu.make_async_copy(grads_ref, own_out, load_sem.at[2]),
        pltpu.make_async_copy(qout_ref, fac_out, load_sem.at[3]),
    ]
    for load in loads:
        load.start()

    barrier = pltpu.get_barrier_semaphore()
    for step in range(1, groups):
        pl.semaphore_signal(
            barrier, inc=1, device_id={"pb": lax.rem(g + step, groups)}, device_id_type=MESH
        )
    for step in range(1, widths):
        pl.semaphore_signal(
            barrier, inc=1, device_id={"wa": lax.rem(w + step, widths)}, device_id_type=MESH
        )
    pl.semaphore_wait(barrier, groups + widths - 2)

    sources = (acts_ref, grads_ref)
    tokens = (tok_in, tok_out)

    def send_own(kind, chunk, slot, target):
        span = pl.ds(chunk * rows, rows)
        for half_at in range(2):
            pltpu.make_async_remote_copy(
                src_ref=sources[half_at].at[span],
                dst_ref=tokens[half_at].at[slot - 1, span],
                send_sem=own_send.at[half_at, kind],
                recv_sem=tok_recv.at[half_at, slot - 1, chunk],
                device_id={"pb": target},
                device_id_type=MESH,
            ).start()

    def own_done(kind):
        for half_at in range(2):
            pltpu.make_async_copy(
                sources[half_at], sources[half_at], own_send.at[half_at, kind]
            ).wait()

    def send_on(chunk, slot, sem, slot_there, target):
        span = pl.ds(chunk * rows, rows)
        for half_at in range(2):
            pltpu.make_async_remote_copy(
                src_ref=tokens[half_at].at[slot - 1, span],
                dst_ref=tokens[half_at].at[slot_there - 1, span],
                send_sem=sem(half_at),
                recv_sem=tok_recv.at[half_at, slot_there - 1, chunk],
                device_id={"pb": target},
                device_id_type=MESH,
            ).start()

    def direct_next(j):
        if j == 1:
            return jnp.logical_or(even_core, jnp.logical_not(odd_chip))
        return None

    for chunk in range(chunks):
        @pl.when(jnp.logical_not(even_core))
        def _():
            send_own(0, chunk, window - 1, device(chip + half, 0))

        for j in range(1, half):
            condition = direct_next(j)
            if condition is None:
                send_own(j, chunk, 2 * j, device(chip + j, core))
            else:
                @pl.when(condition)
                def _():
                    send_own(j, chunk, 2 * j, device(chip + j, core))

        @pl.when(even_core)
        def _():
            send_own(0, chunk, 1, partner)

    def wait_for(ref, sem):
        pltpu.make_async_copy(ref, ref, sem).wait()

    def split(depth):
        piece = depth
        while piece > 1024 and piece % 256 == 0:
            piece //= 2
        return piece

    def project(left, fac, place, column):
        depth = fac.shape[0]
        piece = split(depth)

        def body(i, total):
            span = pl.ds(pl.multiple_of(i * piece, piece), piece)
            return total + jnp.dot(
                left(span), fac[span, :], preferred_element_type=jnp.float32
            )

        part[place, :, column:column + cols] = lax.fori_loop(
            0, depth // piece, body, jnp.zeros((rows, cols), jnp.float32)
        )

    def exchange(place):
        for step in range(1, widths):
            peer = lax.rem(w + step, widths)
            pltpu.make_async_remote_copy(
                src_ref=part.at[place, pl.ds(pl.multiple_of(peer * share, share), share)],
                dst_ref=got.at[place, step - 1],
                send_sem=part_send.at[place],
                recv_sem=part_recv.at[place],
                device_id={"wa": peer},
                device_id_type=MESH,
            ).start()

    lengths_float = lengths_ref[...].astype(jnp.float32)

    def settle(place, slot, chunk):
        wait_for(got.at[place], part_recv.at[place])
        total = part[place, pl.ds(pl.multiple_of(w * share, share), share), :]
        for step in range(widths - 1):
            total = total + got[place, step]
        into = pl.ds(pl.multiple_of(place * share, share), share)
        prods[into, :] = total[:, :cols] * total[:, cols:]
        anchor = lax.rem(g - slot + groups, groups)
        first = anchor * tok + chunk * rows + w * share
        spots = first + lax.broadcasted_iota(jnp.int32, (share, nseq), 0)
        table[into, :] = spots

    def own_chunk(chunk, carry):
        span = pl.ds(pl.multiple_of(chunk * rows, rows), rows)
        project(lambda at: own_in[span, at], fac_in, chunk, 0)
        project(lambda at: own_out[span, at], fac_out, chunk, cols)
        exchange(chunk)
        return carry

    for load in loads:
        load.wait()
    lax.fori_loop(0, chunks, own_chunk, 0)

    even_order = [window - 1]
    odd_order = [1]
    for j in range(1, half):
        even_order += [2 * j, 2 * j - 1]
        odd_order += [2 * j, 2 * j + 1]

    def slot_of(p):
        return jnp.where(even_core, even_order[p], odd_order[p])

    relays = jnp.logical_and(even_core, lax.rem(chip - half + chips, 2) == 1)

    def arrived(chunk, carry):
        span = pl.ds(pl.multiple_of(chunk * rows, rows), rows)
        for p in range(slots):
            slot = slot_of(p)
            for half_at in range(2):
                wait_for(
                    tokens[half_at].at[slot - 1, span], tok_recv.at[half_at, slot - 1, chunk]
                )
            if p == 0 and half > 1:
                @pl.when(relays)
                def _():
                    send_on(
                        chunk, slot, lambda at: relay_send.at[at], 2,
                        device(chip - half + 1, 1),
                    )
            if p % 2 == 1:
                there = jnp.where(even_core, p + 2, p)
                send_on(
                    chunk, slot, lambda at: fwd_send.at[at, p // 2], there, partner
                )
            place = chunks + chunk * slots + p
            project(lambda at: tok_in[slot - 1, span, at], fac_in, place, 0)
            project(lambda at: tok_out[slot - 1, span, at], fac_out, place, cols)
            exchange(place)
            if p == 0:
                settle(chunk, 0, chunk)
            else:
                @pl.when(chunk > 0)
                def _():
                    settle(place - slots - 1, slot_of(p - 1), chunk - 1)

        @pl.when(chunk > 0)
        def _():
            settle(chunks + chunk * slots - 1, slot_of(slots - 1), chunk - 1)

        return carry

    lax.fori_loop(0, chunks, arrived, 0)
    for p in range(slots):
        settle(chunks + (chunks - 1) * slots + p, slot_of(p), chunks - 1)

    upto = (
        lax.broadcasted_iota(jnp.int32, (nseq, nseq), 0)
        <= lax.broadcasted_iota(jnp.int32, (nseq, nseq), 1)
    ).astype(jnp.float32)
    wide = jnp.broadcast_to(lengths_float, (8, nseq))
    ends = jnp.dot(
        wide, upto, precision=HIGHEST, preferred_element_type=jnp.float32
    )[0:1, :].astype(jnp.int32)
    starts = ends - lengths_ref[...]
    spots = table[...]
    inside = ((spots >= starts) & (spots < ends)).astype(jnp.float32)
    local_q = cols // RANK
    chooses = (
        lax.broadcasted_iota(jnp.int32, (local_q, cols), 1) // RANK
        == lax.broadcasted_iota(jnp.int32, (local_q, cols), 0)
    ).astype(jnp.float32)
    scores = lax.dot_general(
        chooses, prods[...], (((1,), (1,)), ((), ())),
        precision=HIGHEST, preferred_element_type=jnp.float32,
    )
    tot[...] = jnp.dot(
        scores, inside, precision=HIGHEST, preferred_element_type=jnp.float32
    )
    for step in range(1, widths):
        pltpu.make_async_remote_copy(
            src_ref=tot,
            dst_ref=tot_got.at[step - 1],
            send_sem=tot_send.at[step - 1],
            recv_sem=tot_recv.at[step - 1],
            device_id={"wa": lax.rem(w + step, widths)},
            device_id_type=MESH,
        ).start()

    own_done_needed = [(0, None)]
    own_done(0)
    for j in range(1, half):
        condition = direct_next(j)
        if condition is None:
            own_done(j)
        else:
            @pl.when(condition)
            def _():
                own_done(j)
        for half_at in range(2):
            wait_for(tokens[half_at].at[0], fwd_send.at[half_at, j - 1])
    if half > 1:
        @pl.when(relays)
        def _():
            for half_at in range(2):
                wait_for(tokens[half_at].at[0], relay_send.at[half_at])

    def part_done(place, carry):
        wait_for(got.at[place], part_send.at[place])
        return carry

    lax.fori_loop(0, chunks * window, part_done, 0)

    total = tot[...]
    for step in range(widths - 1):
        wait_for(tot_got.at[step], tot_recv.at[step])
        total = total + tot_got[step]
    for step in range(widths - 1):
        wait_for(tot, tot_send.at[step])
    out_ref[...] = total / lengths_float


def shards(groups, widths, acts, grads, query_in, query_out, lengths):
    tok, d_in = acts.shape
    d_out = grads.shape[1]
    cols = query_in.shape[1]
    nseq = lengths.shape[0]
    window = groups // 2
    half = window // 2
    chunks = max(1, min(4, tok // (8 * widths)))
    rows = tok // chunks
    share = rows // widths
    slots = window - 1
    places = chunks * window
    local_q = cols // RANK
    bf16, f32 = jnp.bfloat16, jnp.float32
    dma = pltpu.SemaphoreType.DMA
    vmem = pltpu.VMEM
    whole = pl.BlockSpec(memory_space=pl.ANY)
    full = pl.pallas_call(
        functools.partial(kernel, groups, widths, chunks),
        out_shape=jax.ShapeDtypeStruct((local_q, nseq), f32),
        in_specs=[whole] * 4 + [pl.BlockSpec(memory_space=pltpu.VMEM)],
        out_specs=pl.BlockSpec(memory_space=pltpu.VMEM),
        scratch_shapes=[
            vmem((tok, d_in), bf16),
            vmem((tok, d_out), bf16),
            vmem((d_in, cols), bf16),
            vmem((d_out, cols), bf16),
            vmem((slots, tok, d_in), bf16),
            vmem((slots, tok, d_out), bf16),
            vmem((places, rows, 2 * cols), f32),
            vmem((places, widths - 1, share, 2 * cols), f32),
            vmem((places * share, cols), f32),
            vmem((places * share, nseq), jnp.int32),
            vmem((local_q, nseq), f32),
            vmem((widths - 1, local_q, nseq), f32),
            dma((4,)),
            dma((2, max(half, 1))),
            dma((2, max(half - 1, 1))),
            dma((2,)),
            dma((2, slots, chunks)),
            dma((places,)),
            dma((places,)),
            dma((widths - 1,)),
            dma((widths - 1,)),
        ],
        compiler_params=pltpu.CompilerParams(
            collective_id=0, has_side_effects=True, vmem_limit_bytes=60 << 20
        ),
    )(acts, grads, query_in, query_out, lengths.reshape(1, nseq))
    seqs = nseq // widths
    return lax.dynamic_slice_in_dim(full, lax.axis_index("wa") * seqs, seqs, 1)


def solution(mesh):
    return jax.shard_map(
        functools.partial(shards, mesh.shape["pb"], mesh.shape["wa"]),
        mesh=mesh,
        in_specs=(P("pb", "wa"), P("pb", "wa"), P("wa", "pb"), P("wa", "pb"), P()),
        out_specs=P("pb", "wa"),
        check_vma=False,
    )
```

time: 267 us -> 148 us (0.55)
  waiting for transfers between devices: 185 us -> 0 us
  Pallas kernels: 0 us -> 147 us
  matrix products: 36.7 us -> 0 us
  local copies, waits for them, and re-layouts: 19.4 us -> 1.38 us
  between operations: 15.1 us -> 0.01 us
  starting transfers between devices: 5.54 us -> 0 us
  other arithmetic: 4.99 us -> 0 us
    reduce_scatter x8 -> x0, waiting for transfers between devices: 152 us -> none  [the longest x4 89.4 us: settle_step(): lax.psum_scatter(proj_in, 'wa', scatter_dimension=0, tiled=True)]
    pallas_call x0 -> x1, Pallas kernels: none -> 147 us  [shards(): pl.pallas_call(functools.partial(kernel, groups, widths, chunks), out_sha...]
    dot_general x12 -> x0, matrix products: 36.7 us -> none  [the longest x4 28.3 us: project(): jnp.dot(held[0], held[2], preferred_element_type=jnp.float32)]
    unnamed x4 -> x0, waiting for transfers between devices: 17.6 us -> none
    ppermute x6 -> x0, waiting for transfers between devices: 14.9 us -> none  [shifted(): return lax.ppermute(value, axis, pairs)]
    while x12 -> x0, local copies, waits for them, and re-layouts: 13 us -> none
    unnamed x8 -> x0, local copies, waits for them, and re-layouts: 5.79 us -> none
    ppermute x6 -> x0, starting transfers between devices: 5.27 us -> none  [shifted(): return lax.ppermute(value, axis, pairs)]
  transfers between devices with their start and end apart: 15 -> 0, of which waited for: 12 -> 0; matrix products, arithmetic and copies ran while one was open for 14% -> 0% of each run, Pallas kernels for 0% -> 0%
where the time goes in v1:
time: 148 us
  Pallas kernels  147 us (99%)
    pallas_call x1, Pallas kernels, shards(): pl.pallas_call(functools.partial(kernel, groups, widths, chunks), out_sha...  147 us

profile of v1, /device:TPU:0, one launch (start us, length us, event | category | flops | bytes accessed | tf_op | source)
XLA Modules:
  0.0 148.2 jit_solution(5739761963261930896)
XLA Ops:
  0.0 146.8 %shard_map.55 = f32[16,128]{1,0:T(8,128)} custom-call(bf16[256,7168]{1,0:T(8,128)(2,1)} %acts_ref.1, bf16[256,2048]{1,0:T(8,128)(2,1)} %grads_ref.1, bf16[7168,512]{1,0:T(8,128)(2,1)} %qin_ref.1, bf16[2048,512]{1,0:T(8,128)(2,1)} %qout_ref.1, s32[1,128]{1,0:T(1,128)} %bitcast.1), custom_call_target="tpu_custom_call" | custom-call | tf_op jit(solution)/shard_map/pallas_call | solution.py:317
  146.8 1.4 constant_dynamic-slice_fusion

commit v2 on v1

--- a/solution.py
+++ b/solution.py
@@ -26,10 +26,10 @@
     half = window // 2
     tok = acts_ref.shape[0]
     rows = tok // chunks
-    share = rows // widths
     cols = qin_ref.shape[1]
     nseq = lengths_ref.shape[1]
     slots = window - 1
+    lag = 3
 
     g = lax.axis_index("pb")
     w = lax.axis_index("wa")
@@ -67,7 +67,7 @@
     tokens = (tok_in, tok_out)
 
     def send_own(kind, chunk, slot, target):
-        span = pl.ds(chunk * rows, rows)
+        span = pl.ds(pl.multiple_of(chunk * rows, rows), rows)
         for half_at in range(2):
             pltpu.make_async_remote_copy(
                 src_ref=sources[half_at].at[span],
@@ -85,7 +85,7 @@
             ).wait()
 
     def send_on(chunk, slot, sem, slot_there, target):
-        span = pl.ds(chunk * rows, rows)
+        span = pl.ds(pl.multiple_of(chunk * rows, rows), rows)
         for half_at in range(2):
             pltpu.make_async_remote_copy(
                 src_ref=tokens[half_at].at[slot - 1, span],
@@ -128,7 +128,7 @@
             piece //= 2
         return piece
 
-    def project(left, fac, place, column):
+    def project(left, fac, at, size, column):
         depth = fac.shape[0]
         piece = split(depth)
 
@@ -138,98 +138,123 @@
                 left(span), fac[span, :], preferred_element_type=jnp.float32
             )
 
-        part[place, :, column:column + cols] = lax.fori_loop(
-            0, depth // piece, body, jnp.zeros((rows, cols), jnp.float32)
+        part[at:at + size, column:column + cols] = lax.fori_loop(
+            0, depth // piece, body, jnp.zeros((size, cols), jnp.float32)
         )
 
     def exchange(place):
+        at, size = steps[place][:2]
+        share = size // widths
         for step in range(1, widths):
             peer = lax.rem(w + step, widths)
             pltpu.make_async_remote_copy(
-                src_ref=part.at[place, pl.ds(pl.multiple_of(peer * share, share), share)],
-                dst_ref=got.at[place, step - 1],
+                src_ref=part.at[pl.ds(pl.multiple_of(at + peer * share, share), share)],
+                dst_ref=got.at[step - 1, pl.ds(at // widths, share)],
                 send_sem=part_send.at[place],
                 recv_sem=part_recv.at[place],
                 device_id={"wa": peer},
                 device_id_type=MESH,
             ).start()
 
+    def parcel(place):
+        at, size = steps[place][:2]
+        return got.at[:, pl.ds(at // widths, size // widths)]
+
     lengths_float = lengths_ref[...].astype(jnp.float32)
 
-    def settle(place, slot, chunk):
-        wait_for(got.at[place], part_recv.at[place])
-        total = part[place, pl.ds(pl.multiple_of(w * share, share), share), :]
+    def settle(place):
+        at, size, slot, row = steps[place]
+        share = size // widths
+        wait_for(parcel(place), part_recv.at[place])
+        total = part[pl.ds(pl.multiple_of(at + w * share, share), share), :]
+        into = slice(at // widths, at // widths + share)
         for step in range(widths - 1):
-            total = total + got[place, step]
-        into = pl.ds(pl.multiple_of(place * share, share), share)
+            total = total + got[step, into, :]
         prods[into, :] = total[:, :cols] * total[:, cols:]
         anchor = lax.rem(g - slot + groups, groups)
-        first = anchor * tok + chunk * rows + w * share
-        spots = first + lax.broadcasted_iota(jnp.int32, (share, nseq), 0)
-        table[into, :] = spots
-
-    def own_chunk(chunk, carry):
-        span = pl.ds(pl.multiple_of(chunk * rows, rows), rows)
-        project(lambda at: own_in[span, at], fac_in, chunk, 0)
-        project(lambda at: own_out[span, at], fac_out, chunk, cols)
-        exchange(chunk)
-        return carry
+        first = anchor * tok + row + w * share
+        table[into, :] = first + lax.broadcasted_iota(jnp.int32, (share, nseq), 0)
+
+    span_of = range(chunks)
+    direct = [2 * j for j in range(1, half)]
+    even_chip_even = [(k, c) for k in direct for c in span_of]
+    for c in span_of:
+        even_chip_even += [(window - 1, c)] + [(k - 1, c) for k in direct]
+    even_chip_odd = [(1, c) for c in span_of]
+    even_chip_odd += [(k + 1, c) for k in direct for c in span_of]
+    even_chip_odd += [(k, c) for k in direct for c in span_of]
+
+    def woven(first, other):
+        order = []
+        for c in span_of:
+            order += [(first, at) for at in (2 * c, 2 * c + 1) if at < chunks]
+            for k in direct:
+                order += [(k, c), (k + other, c)]
+        return order
+
+    odd_chip_even = woven(window - 1, -1)
+    odd_chip_odd = woven(1, 1)
+
+    def role(step, field):
+        return jnp.where(
+            odd_chip,
+            jnp.where(even_core, odd_chip_even[step][field], odd_chip_odd[step][field]),
+            jnp.where(even_core, even_chip_even[step][field], even_chip_odd[step][field]),
+        )
+
+    steps = []
+    own_rows = tok // 2
+    for i in range(2):
+        steps.append((i * own_rows, own_rows, 0, i * own_rows))
+    for i in range(slots * chunks):
+        steps.append((tok + i * rows, rows, role(i, 0), role(i, 1) * rows))
 
     for load in loads:
         load.wait()
-    lax.fori_loop(0, chunks, own_chunk, 0)
-
-    even_order = [window - 1]
-    odd_order = [1]
-    for j in range(1, half):
-        even_order += [2 * j, 2 * j - 1]
-        odd_order += [2 * j, 2 * j + 1]
-
-    def slot_of(p):
-        return jnp.where(even_core, even_order[p], odd_order[p])
+    for i in range(2):
+        span = pl.ds(i * own_rows, own_rows)
+        project(lambda at: own_in[span, at], fac_in, i * own_rows, own_rows, 0)
+        project(lambda at: own_out[span, at], fac_out, i * own_rows, own_rows, cols)
+        exchange(i)
 
     relays = jnp.logical_and(even_core, lax.rem(chip - half + chips, 2) == 1)
 
-    def arrived(chunk, carry):
+    for i in range(slots * chunks):
+        slot, chunk = role(i, 0), role(i, 1)
         span = pl.ds(pl.multiple_of(chunk * rows, rows), rows)
-        for p in range(slots):
-            slot = slot_of(p)
-            for half_at in range(2):
-                wait_for(
-                    tokens[half_at].at[slot - 1, span], tok_recv.at[half_at, slot - 1, chunk]
+        for half_at in range(2):
+            wait_for(
+                tokens[half_at].at[slot - 1, span], tok_recv.at[half_at, slot - 1, chunk]
+            )
+        if half > 1:
+            @pl.when(jnp.logical_and(relays, slot == window - 1))
+            def _():
+                send_on(
+                    chunk, slot, lambda at: relay_send.at[at], 2,
+                    device(chip - half + 1, 1),
                 )
-            if p == 0 and half > 1:
-                @pl.when(relays)
-                def _():
-                    send_on(
-                        chunk, slot, lambda at: relay_send.at[at], 2,
-                        device(chip - half + 1, 1),
-                    )
-            if p % 2 == 1:
-                there = jnp.where(even_core, p + 2, p)
+
+            @pl.when(lax.rem(slot, 2) == 0)
+            def _():
+                there = jnp.where(even_core, slot + 1, slot - 1)
                 send_on(
-                    chunk, slot, lambda at: fwd_send.at[at, p // 2], there, partner
+                    chunk, slot, lambda at: fwd_send.at[at, slot // 2 - 1], there, partner
                 )
-            place = chunks + chunk * slots + p
-            project(lambda at: tok_in[slot - 1, span, at], fac_in, place, 0)
-            project(lambda at: tok_out[slot - 1, span, at], fac_out, place, cols)
-            exchange(place)
-            if p == 0:
-                settle(chunk, 0, chunk)
-            else:
-                @pl.when(chunk > 0)
-                def _():
-                    settle(place - slots - 1, slot_of(p - 1), chunk - 1)
-
-        @pl.when(chunk > 0)
-        def _():
-            settle(chunks + chunk * slots - 1, slot_of(slots - 1), chunk - 1)
-
-        return carry
-
-    lax.fori_loop(0, chunks, arrived, 0)
-    for p in range(slots):
-        settle(chunks + (chunks - 1) * slots + p, slot_of(p), chunks - 1)
+        at, size = steps[2 + i][:2]
+        project(lambda to: tok_in[slot - 1, span, to], fac_in, at, size, 0)
+        project(lambda to: tok_out[slot - 1, span, to], fac_out, at, size, cols)
+        exchange(2 + i)
+        if i >= lag:
+            settle(2 + i - lag)
+        if i == lag:
+            settle(0)
+            settle(1)
+
+    for i in range(max(0, slots * chunks - lag), slots * chunks):
+        settle(2 + i)
+    if slots * chunks <= lag:
+        settle(0)
+        settle(1)
 
     upto = (
         lax.broadcasted_iota(jnp.int32, (nseq, nseq), 0)
@@ -264,7 +289,6 @@
             device_id_type=MESH,
         ).start()
 
-    own_done_needed = [(0, None)]
     own_done(0)
     for j in range(1, half):
         condition = direct_next(j)
@@ -282,11 +306,8 @@
             for half_at in range(2):
                 wait_for(tokens[half_at].at[0], relay_send.at[half_at])
 
-    def part_done(place, carry):
-        wait_for(got.at[place], part_send.at[place])
-        return carry
-
-    lax.fori_loop(0, chunks * window, part_done, 0)
+    for place in range(len(steps)):
+        wait_for(parcel(place), part_send.at[place])
 
     total = tot[...]
     for step in range(widths - 1):
@@ -305,10 +326,8 @@
     window = groups // 2
     half = window // 2
     chunks = max(1, min(4, tok // (8 * widths)))
-    rows = tok // chunks
-    share = rows // widths
     slots = window - 1
-    places = chunks * window
+    places = 2 + chunks * slots
     local_q = cols // RANK
     bf16, f32 = jnp.bfloat16, jnp.float32
     dma = pltpu.SemaphoreType.DMA
@@ -326,10 +345,10 @@
             vmem((d_out, cols), bf16),
             vmem((slots, tok, d_in), bf16),
             vmem((slots, tok, d_out), bf16),
-            vmem((places, rows, 2 * cols), f32),
-            vmem((places, widths - 1, share, 2 * cols), f32),
-            vmem((places * share, cols), f32),
-            vmem((places * share, nseq), jnp.int32),
+            vmem((window * tok, 2 * cols), f32),
+            vmem((widths - 1, window * tok // widths, 2 * cols), f32),
+            vmem((window * tok // widths, cols), f32),
+            vmem((window * tok // widths, nseq), jnp.int32),
             vmem((local_q, nseq), f32),
             vmem((widths - 1, local_q, nseq), f32),
             dma((4,)),

time: 148 us -> 130 us (0.88)
  Pallas kernels: 147 us -> 129 us
    pallas_call x1, Pallas kernels: 147 us -> 129 us  [shards(): pl.pallas_call(functools.partial(kernel, groups, widths, chunks), out_sha...]
where the time goes in v2:
time: 130 us
  Pallas kernels  129 us (99%)
  local copies, waits for them, and re-layouts  1.38 us (1%)
    pallas_call x1, Pallas kernels, shards(): pl.pallas_call(functools.partial(kernel, groups, widths, chunks), out_sha...  129 us

profile of v2, /device:TPU:0, one launch (start us, length us, event | category | flops | bytes accessed | tf_op | source)
XLA Modules:
  0.0 130.0 jit_solution(15365077350206202706)
XLA Ops:
  0.0 128.7 %shard_map.55 = f32[16,128]{1,0:T(8,128)} custom-call(bf16[256,7168]{1,0:T(8,128)(2,1)} %acts_ref.1, bf16[256,2048]{1,0:T(8,128)(2,1)} %grads_ref.1, bf16[7168,512]{1,0:T(8,128)(2,1)} %qin_ref.1, bf16[2048,512]{1,0:T(8,128)(2,1)} %qout_ref.1, s32[1,128]{1,0:T(1,128)} %bitcast.1), custom_call_target="tpu_custom_call" | custom-call | tf_op jit(solution)/shard_map/pallas_call | solution.py:336
  128.7 1.4 %constant_dynamic-slice_fusion = f32[16,32]{1,0:T(8,128)} fusion(f32[16,128]{1,0:T(8,128)} %shard_map.55, s32[]{:T(128)S(6)} %select_n.3), kind=kLoop, calls=%fused_computation | loop fusion | bytes 4100 | tf_op jit(solution)/shard_map/dynamic_slice | solution.py:369
